TPU v7x, 32 devices: a whole 2x2x4 slice. The times are simulated.
32 devices in a mesh: groups: 2 (over y), ctx: 4 (over z), tp: 2 (over x), sub: 2 (over core).
Axes of the slice: x: 2, y: 2, z: 4, core: 2. Of those that a mesh axis runs over, the one named last changes fastest.
Arguments:
- queries: bfloat16 [3072, 8192], P(('groups', 'ctx'), ('tp', 'sub')), parts along dimension 0, may hold values from -200 to 200
- keys: bfloat16 [3072, 1024], P(('groups', 'ctx'), ('tp', 'sub')), parts along dimension 0, may hold values from -6 to 6
- values: bfloat16 [3072, 1024], P(('groups', 'ctx'), ('tp', 'sub')), parts along dimension 0, may hold values from -6 to 6
- segment_ids: int32 [3072], P(('groups', 'ctx')), parts along dimension 0, may hold values from 0 to 8, as said below
Outputs:
- attended: bfloat16 [3072, 8192], P(('groups', 'ctx'), ('tp', 'sub')), parts along dimension 0
There are 2 independent parts, one for each index of `groups`. A program takes and returns all parts, laid end to end along the dimension named above; each array names one. Nothing has to cross between parts.
Inputs may be any that keep to these rules, and one draw needn't show every extreme that they name: segment_ids is 0 on the first 384 tokens; after them exactly 8 chains 1, 2, ..., 8 follow in order and fill the row, each a run of 96 to 192 tokens, one of them exactly 192.
All inputs are finite; a program needn't handle non-finite values.
Results may differ from a plain program's by a relative error of at most 0.0041.
Values may be sent and summed in bfloat16 or wider, within the bound.
No kernel may reach another device: no remote copies, remote signals or barrier semaphores. Data moves between devices by JAX's collectives and lax.ppermute only.
A program may use at most 64 MiB of HBM per device.

v0:
```python
import jax
import jax.numpy as jnp
from jax import lax
from jax.sharding import PartitionSpec as P

HEAD_DIM = 128
GROUP = 8


def attend_block(
    running,
    key_block,
    value_block,
    segment_block,
    first_row,
    query_heads,
    query_places,
    query_segment,
):
    number = key_block.shape[0]
    heads_here = key_block.shape[1] // HEAD_DIM
    key_places = first_row + jnp.arange(number, dtype=jnp.int32)
    same = (segment_block[None, :] == query_segment[:, None]) | (segment_block[None, :] == 0)
    visible = (key_places[None, :] <= query_places[:, None]) & same
    key_heads = key_block.reshape(number, heads_here, HEAD_DIM)
    value_heads = value_block.reshape(number, heads_here, HEAD_DIM)

    def compute(state):
        row_peak, row_total, weighted = state
        scores = jnp.einsum(
            "qhgd,khd->hgqk", query_heads, key_heads, preferred_element_type=jnp.float32
        ) * HEAD_DIM ** (-0.5)
        scores = jnp.where(visible[None, None], scores, -1e30)
        new_peak = jnp.maximum(row_peak, jnp.max(scores, axis=-1))
        factor = jnp.exp(row_peak - new_peak)
        weights = jnp.where(visible[None, None], jnp.exp(scores - new_peak[..., None]), 0.0)
        new_total = row_total * factor + jnp.sum(weights, axis=-1)
        added = jnp.einsum(
            "hgqk,khd->hgqd",
            weights.astype(jnp.bfloat16),
            value_heads,
            preferred_element_type=jnp.float32,
        )
        return (new_peak, new_total, weighted * factor[..., None] + added)

    return lax.cond(jnp.any(visible), compute, lambda state: state, running)


def per_device(queries, keys, values, segment_ids):
    row_count = queries.shape[0]
    heads_here = keys.shape[1] // HEAD_DIM
    my_index = lax.axis_index("ctx")
    query_places = my_index * row_count + jnp.arange(row_count, dtype=jnp.int32)
    query_heads = queries.reshape(row_count, heads_here, GROUP, HEAD_DIM)
    initial = (
        jnp.full((heads_here, GROUP, row_count), -1e30, jnp.float32),
        jnp.zeros((heads_here, GROUP, row_count), jnp.float32),
        jnp.zeros((heads_here, GROUP, row_count, HEAD_DIM), jnp.float32),
    )
    key_all = lax.all_gather(keys, "ctx", axis=0, tiled=True)
    value_all = lax.all_gather(values, "ctx", axis=0, tiled=True)
    segment_all = lax.all_gather(segment_ids, "ctx", axis=0, tiled=True)
    blocks = max(1, key_all.shape[0] // row_count)
    width_rows = key_all.shape[0] // blocks

    def turn(number, state):
        offset = number * width_rows
        key_part = lax.dynamic_slice_in_dim(key_all, offset, width_rows, 0)
        value_part = lax.dynamic_slice_in_dim(value_all, offset, width_rows, 0)
        segment_part = lax.dynamic_slice_in_dim(segment_all, offset, width_rows, 0)
        return attend_block(
            state,
            key_part,
            value_part,
            segment_part,
            offset,
            query_heads,
            query_places,
            segment_ids,
        )

    final = lax.fori_loop(0, blocks, turn, initial)
    row_peak, row_total, weighted = final
    mixed = weighted / row_total[..., None]
    mixed = jnp.transpose(mixed, (2, 0, 1, 3)).reshape(row_count, heads_here * GROUP * HEAD_DIM)
    return mixed.astype(jnp.bfloat16)


def solution(mesh):
    placed = (
        P(("groups", "ctx"), ("tp", "sub")),
        P(("groups", "ctx"), ("tp", "sub")),
        P(("groups", "ctx"), ("tp", "sub")),
        P(("groups", "ctx")),
    )
    return jax.shard_map(
        per_device,
        mesh=mesh,
        in_specs=placed,
        out_specs=P(("groups", "ctx"), ("tp", "sub")),
        check_vma=False,
    )
```

profile of v0, /device:TPU:22, one launch (start us, length us, event | category | flops | bytes accessed | tf_op | source)
XLA Modules:
  0.0 98.1 jit_solution(1589817121826386383)
XLA Ops:
  0.0 0.7 reshape.39
  0.7 10.3 %all-gather = s32[4,1,384]{2,1,0:T(1,128)S(1)} all-gather(s32[1,1,384]{2,1,0:T(1,128)S(1)} %reshape.39), channel_id=1, replica_groups=mesh['groups'=2,'ctx'=4,'tp'=2,'sub'=2] {'ctx'}, dimensions={0}, use_global_device_ids=true | all-gather | bytes 7680 | tf_op jit(solution)/shard_map/all_gather | solution.py:62
  11.0 1.1 %copy.18 = bf16[384,256]{0,1:T(8,128)(2,1)S(1)} copy(bf16[384,256]{1,0:T(8,128)(2,1)} %param.9) | data formatting | bytes 393216 | tf_op args[1]
  12.1 1.1 %copy.20 = bf16[384,256]{0,1:T(8,128)(2,1)S(1)} copy(bf16[384,256]{1,0:T(8,128)(2,1)} %param.10) | data formatting | bytes 393216 | tf_op args[2]
  13.2 18.8 %all_gather.11 = bf16[1536,256]{0,1:T(8,128)(2,1)} all-gather(bf16[384,256]{0,1:T(8,128)(2,1)S(1)} %copy.20), channel_id=1, replica_groups=mesh['groups'=2,'ctx'=4,'tp'=2,'sub'=2] {'ctx'}, dimensions={0}, use_global_device_ids=true | all-gather | bytes 983040 | tf_op jit(solution)/shard_map/all_gather | solution.py:61
  32.0 17.9 %all_gather.10 = bf16[1536,256]{0,1:T(8,128)(2,1)} all-gather(bf16[384,256]{0,1:T(8,128)(2,1)S(1)} %copy.18), channel_id=1, replica_groups=mesh['groups'=2,'ctx'=4,'tp'=2,'sub'=2] {'ctx'}, dimensions={0}, use_global_device_ids=true | all-gather | bytes 983040 | tf_op jit(solution)/shard_map/all_gather | solution.py:60
  49.9 1.9 %copy.19 = bf16[384,2048]{0,1:T(8,128)(2,1)S(1)} copy(bf16[384,2048]{1,0:T(8,128)(2,1)} %param.8) | data formatting | bytes 3145728 | tf_op args[0]
  51.8 1.0 copy.21
  52.8 2.0 %broadcast_in_dim.53 = f32[2,8,384,128]{3,2,1,0:T(8,128)} broadcast(f32[]{:T(128)} %constant.68.clone.1), dimensions={} | broadcast | bytes 3145732 | tf_op jit(solution)/shard_map/broadcast_in_dim | solution.py:58
  54.8 0.0 copy-done.2
  54.8 38.4 %while.18 = (s32[]{:T(128)}, f32[2,8,384]{2,1,0:T(8,128)S(1)}, f32[2,8,384]{2,1,0:T(8,128)S(1)}, f32[2,8,384,128]{3,2,1,0:T(8,128)}, s32[1536]{0:T(1024)S(1)}, /...) while((s32[]{:T(128)}, f32[2,8,384]{2,1,0:T(8,128)S(1)}, ...), condition=%wide.region_6.7_spmd.clone, body=%wide.region_0.6_spmd.clone.sunk | while | flops 1240953984 | bytes 63517816 | solution.py:82
  54.8 0.1 broadcast_compare_fusion.2
  54.9 0.9 fusion.19
  56.4 10.6 %conditional.3 = ((f32[2,8,384]{2,1,0:T(8,128)S(1)}, f32[2,8,384]{2,1,0:T(8,128)S(1)}, f32[2,8,384,128]{3,2,1,0:T(8,128)})) conditional(s32[]{:T(128)} %convert_element_type.33, (f32[2,8,384]{2,1,0:T(8,128)S(1)}, f32[2,8,384]{2,1,0:T(8,128)S(1)}, f32[2,8,384,128]{3,2,1,0:T(8,128)}) %tuple.60, (pred[384,384]{0,1:T(8,128)(4,1)S(1)}, ...), branch_computations={%region_2.0_spmd, %region_3.5_spmd} | conditional | flops 1240215552 | bytes 63357020 | solution.py:46
  56.4 1.1 %constant_dynamic-slice_fusion = (bf16[384,256]{0,1:T(8,128)(2,1)S(1)}, bf16[384,256]{0,1:T(8,128)(2,1)S(1)}) fusion(bf16[1536,256]{0,1:T(8,128)(2,1)} %get-tuple-element.240, s32[]{:T(128)} %get-tuple-element.236, bf16[1536,256]{0,1:T(8,128)(2,1)} %get-tuple-element.235), kind=kLoop, calls=%fused_computation.11 | loop fusion | bytes 786436 | tf_op jit(solution)/shard_map/while/body/eval_jaxpr/dynamic_slice | solution.py:69
  57.5 1.7 %fusion.2 = (f32[2,8,384]{2,1,0:T(8,128)S(1)}, f32[2,384,384,8]{2,1,3,0:T(8,128)S(1)}) fusion(pred[384,384]{0,1:T(8,128)(4,1)S(1)} %get-tuple-element.234, bf16[384,2,128,1]{0,2,3,1:T(8,128)(2,1)S(1)} %bitcast.34, bf16[384,2,8,128]{3,0,2,1:T(8,128)(2,1)S(1)} %get-tuple-element.237), kind=kOutput, calls=%fused_computation.3 | convolution fusion | flops 611051520 | bytes 11378688 | tf_op jit(solution)/shard_map/while/body/eval_jaxpr/cond/branch_1_fun/qhgd,khd->hgqk/dot_general | solution.py:30
  59.2 0.0 copy-start
  59.2 2.3 %fusion.4 = f32[2,8,384]{2,1,0:T(8,128)S(1)} fusion(f32[2,384,384,8]{2,1,3,0:T(8,128)S(1)} %get-tuple-element.332, f32[2,8,384]{2,1,0:T(8,128)S(1)} %max.4, pred[384,384]{0,1:T(8,128)(4,1)S(1)} %get-tuple-element.234), kind=kLoop, calls=%fused_computation.5 | loop fusion | flops 11790336 | bytes 9633792 | tf_op jit(solution)/shard_map/while/body/eval_jaxpr/cond/branch_1_fun/reduce_sum | solution.py:37
  61.5 0.0 copy-done
  61.5 3.8 %multiply_add_fusion = f32[2,8,384,128]{3,2,1,0:T(8,128)S(1)} fusion(f32[2,8,384,128]{3,2,1,0:T(8,128)S(1)} %copy-done, bf16[384,2,128,1]{0,2,3,1:T(8,128)(2,1)S(1)} %bitcast.37, f32[2,384,384,8]{2,1,3,0:T(8,128)S(1)} %get-tuple-element.332, f32[2,8,384]{2,1,0:T(8,128)S(1)} %max.4, pred[384,384]{0,1:T(8,128)(4,1)S(1)} %get-tuple-element.234, ...), kind=kOutput, calls=%fused_computation.8 | convolution fusion | flops 617349120 | bytes 16121856 | tf_op jit(solution)/shard_map/while/body/eval_jaxpr/cond/branch_1_fun/hgqk,khd->hgqd/dot_general | solution.py:38
  65.4 0.0 copy-start.1
  65.4 1.6 %copy-done.1 = f32[2,8,384,128]{3,2,1,0:T(8,128)} copy-done((f32[2,8,384,128]{3,2,1,0:T(8,128)}, f32[2,8,384,128]{3,2,1,0:T(8,128)S(1)}, u32[]{:S(2)}) %copy-start.1) | copy-done | bytes 3145752 | tf_op jit(solution)/shard_map/while/body/eval_jaxpr/cond
  67.0 0.1 broadcast_compare_fusion.2
  67.1 0.9 fusion.19
  68.6 10.6 %conditional.3 = ((f32[2,8,384]{2,1,0:T(8,128)S(1)}, f32[2,8,384]{2,1,0:T(8,128)S(1)}, f32[2,8,384,128]{3,2,1,0:T(8,128)})) conditional(s32[]{:T(128)} %convert_element_type.33, (f32[2,8,384]{2,1,0:T(8,128)S(1)}, f32[2,8,384]{2,1,0:T(8,128)S(1)}, f32[2,8,384,128]{3,2,1,0:T(8,128)}) %tuple.60, (pred[384,384]{0,1:T(8,128)(4,1)S(1)}, ...), branch_computations={%region_2.0_spmd, %region_3.5_spmd} | conditional | flops 1240215552 | bytes 63357020 | solution.py:46
  68.6 1.1 %constant_dynamic-slice_fusion = (bf16[384,256]{0,1:T(8,128)(2,1)S(1)}, bf16[384,256]{0,1:T(8,128)(2,1)S(1)}) fusion(bf16[1536,256]{0,1:T(8,128)(2,1)} %get-tuple-element.240, s32[]{:T(128)} %get-tuple-element.236, bf16[1536,256]{0,1:T(8,128)(2,1)} %get-tuple-element.235), kind=kLoop, calls=%fused_computation.11 | loop fusion | bytes 786436 | tf_op jit(solution)/shard_map/while/body/eval_jaxpr/dynamic_slice | solution.py:69
  69.7 1.7 %fusion.2 = (f32[2,8,384]{2,1,0:T(8,128)S(1)}, f32[2,384,384,8]{2,1,3,0:T(8,128)S(1)}) fusion(pred[384,384]{0,1:T(8,128)(4,1)S(1)} %get-tuple-element.234, bf16[384,2,128,1]{0,2,3,1:T(8,128)(2,1)S(1)} %bitcast.34, bf16[384,2,8,128]{3,0,2,1:T(8,128)(2,1)S(1)} %get-tuple-element.237), kind=kOutput, calls=%fused_computation.3 | convolution fusion | flops 611051520 | bytes 11378688 | tf_op jit(solution)/shard_map/while/body/eval_jaxpr/cond/branch_1_fun/qhgd,khd->hgqk/dot_general | solution.py:30
  71.4 0.0 copy-start
  71.5 2.3 %fusion.4 = f32[2,8,384]{2,1,0:T(8,128)S(1)} fusion(f32[2,384,384,8]{2,1,3,0:T(8,128)S(1)} %get-tuple-element.332, f32[2,8,384]{2,1,0:T(8,128)S(1)} %max.4, pred[384,384]{0,1:T(8,128)(4,1)S(1)} %get-tuple-element.234), kind=kLoop, calls=%fused_computation.5 | loop fusion | flops 11790336 | bytes 9633792 | tf_op jit(solution)/shard_map/while/body/eval_jaxpr/cond/branch_1_fun/reduce_sum | solution.py:37
  73.8 0.0 copy-done
  73.8 3.8 %multiply_add_fusion = f32[2,8,384,128]{3,2,1,0:T(8,128)S(1)} fusion(f32[2,8,384,128]{3,2,1,0:T(8,128)S(1)} %copy-done, bf16[384,2,128,1]{0,2,3,1:T(8,128)(2,1)S(1)} %bitcast.37, f32[2,384,384,8]{2,1,3,0:T(8,128)S(1)} %get-tuple-element.332, f32[2,8,384]{2,1,0:T(8,128)S(1)} %max.4, pred[384,384]{0,1:T(8,128)(4,1)S(1)} %get-tuple-element.234, ...), kind=kOutput, calls=%fused_computation.8 | convolution fusion | flops 617349120 | bytes 16121856 | tf_op jit(solution)/shard_map/while/body/eval_jaxpr/cond/branch_1_fun/hgqk,khd->hgqd/dot_general | solution.py:38
  77.6 0.0 copy-start.1
  77.6 1.6 %copy-done.1 = f32[2,8,384,128]{3,2,1,0:T(8,128)} copy-done((f32[2,8,384,128]{3,2,1,0:T(8,128)}, f32[2,8,384,128]{3,2,1,0:T(8,128)S(1)}, u32[]{:S(2)}) %copy-start.1) | copy-done | bytes 3145752 | tf_op jit(solution)/shard_map/while/body/eval_jaxpr/cond
  79.3 0.1 broadcast_compare_fusion.2
  79.4 0.9 fusion.19
  80.9 10.6 %conditional.3 = ((f32[2,8,384]{2,1,0:T(8,128)S(1)}, f32[2,8,384]{2,1,0:T(8,128)S(1)}, f32[2,8,384,128]{3,2,1,0:T(8,128)})) conditional(s32[]{:T(128)} %convert_element_type.33, (f32[2,8,384]{2,1,0:T(8,128)S(1)}, f32[2,8,384]{2,1,0:T(8,128)S(1)}, f32[2,8,384,128]{3,2,1,0:T(8,128)}) %tuple.60, (pred[384,384]{0,1:T(8,128)(4,1)S(1)}, ...), branch_computations={%region_2.0_spmd, %region_3.5_spmd} | conditional | flops 1240215552 | bytes 63357020 | solution.py:46
  80.9 1.1 %constant_dynamic-slice_fusion = (bf16[384,256]{0,1:T(8,128)(2,1)S(1)}, bf16[384,256]{0,1:T(8,128)(2,1)S(1)}) fusion(bf16[1536,256]{0,1:T(8,128)(2,1)} %get-tuple-element.240, s32[]{:T(128)} %get-tuple-element.236, bf16[1536,256]{0,1:T(8,128)(2,1)} %get-tuple-element.235), kind=kLoop, calls=%fused_computation.11 | loop fusion | bytes 786436 | tf_op jit(solution)/shard_map/while/body/eval_jaxpr/dynamic_slice | solution.py:69
  82.0 1.7 %fusion.2 = (f32[2,8,384]{2,1,0:T(8,128)S(1)}, f32[2,384,384,8]{2,1,3,0:T(8,128)S(1)}) fusion(pred[384,384]{0,1:T(8,128)(4,1)S(1)} %get-tuple-element.234, bf16[384,2,128,1]{0,2,3,1:T(8,128)(2,1)S(1)} %bitcast.34, bf16[384,2,8,128]{3,0,2,1:T(8,128)(2,1)S(1)} %get-tuple-element.237), kind=kOutput, calls=%fused_computation.3 | convolution fusion | flops 611051520 | bytes 11378688 | tf_op jit(solution)/shard_map/while/body/eval_jaxpr/cond/branch_1_fun/qhgd,khd->hgqk/dot_general | solution.py:30
  83.7 0.0 copy-start
  83.7 2.3 %fusion.4 = f32[2,8,384]{2,1,0:T(8,128)S(1)} fusion(f32[2,384,384,8]{2,1,3,0:T(8,128)S(1)} %get-tuple-element.332, f32[2,8,384]{2,1,0:T(8,128)S(1)} %max.4, pred[384,384]{0,1:T(8,128)(4,1)S(1)} %get-tuple-element.234), kind=kLoop, calls=%fused_computation.5 | loop fusion | flops 11790336 | bytes 9633792 | tf_op jit(solution)/shard_map/while/body/eval_jaxpr/cond/branch_1_fun/reduce_sum | solution.py:37
  86.0 0.0 copy-done
  86.0 3.8 %multiply_add_fusion = f32[2,8,384,128]{3,2,1,0:T(8,128)S(1)} fusion(f32[2,8,384,128]{3,2,1,0:T(8,128)S(1)} %copy-done, bf16[384,2,128,1]{0,2,3,1:T(8,128)(2,1)S(1)} %bitcast.37, f32[2,384,384,8]{2,1,3,0:T(8,128)S(1)} %get-tuple-element.332, f32[2,8,384]{2,1,0:T(8,128)S(1)} %max.4, pred[384,384]{0,1:T(8,128)(4,1)S(1)} %get-tuple-element.234, ...), kind=kOutput, calls=%fused_computation.8 | convolution fusion | flops 617349120 | bytes 16121856 | tf_op jit(solution)/shard_map/while/body/eval_jaxpr/cond/branch_1_fun/hgqk,khd->hgqd/dot_general | solution.py:38
  89.9 1.6 %copy-done.1 = f32[2,8,384,128]{3,2,1,0:T(8,128)} copy-done((f32[2,8,384,128]{3,2,1,0:T(8,128)}, f32[2,8,384,128]{3,2,1,0:T(8,128)S(1)}, u32[]{:S(2)}) %copy-start.1) | copy-done | bytes 3145752 | tf_op jit(solution)/shard_map/while/body/eval_jaxpr/cond
  91.5 0.1 broadcast_compare_fusion.2
  91.6 0.9 fusion.19
  93.2 2.4 %fusion.13 = bf16[384,2,8,128]{3,0,2,1:T(8,128)(2,1)S(1)} fusion(f32[2,8,384,128]{3,2,1,0:T(8,128)} %get-tuple-element.257, f32[2,8,384]{2,1,0:T(8,128)S(1)} %get-tuple-element.258), kind=kLoop, calls=%fused_computation.22 | loop fusion | flops 1572864 | bytes 4743168 | tf_op jit(solution)/shard_map/convert_element_type | solution.py:86
  95.6 1.0 %copy.22 = bf16[384,2,8,128]{3,2,1,0:T(8,128)(2,1)S(1)} copy(bf16[384,2,8,128]{3,0,2,1:T(8,128)(2,1)S(1)} %fusion.13) | data formatting | bytes 3145728 | tf_op jit(solution)/shard_map/convert_element_type | solution.py:86
  96.6 1.6 %copy.32 = bf16[48,8,16,128]{3,1,2,0:T(8,128)(2,1)} copy(bf16[48,8,16,128]{3,2,1,0:T(8,128)(2,1)S(1)} %bitcast.35) | data formatting | bytes 3145728
  (20 shorter events, 0.1 us)
Async XLA Ops:
  49.9 4.9 %copy-start.2 = (s32[384]{0:T(512)S(1)}, s32[384]{0:T(512)}, u32[]{:S(2)}) copy-start(s32[384]{0:T(512)} %param.11) | copy-start | bytes 4612
  59.2 2.3 %copy-start = (f32[2,8,384,128]{3,2,1,0:T(8,128)S(1)}, f32[2,8,384,128]{3,2,1,0:T(8,128)}, u32[]{:S(2)}) copy-start(f32[2,8,384,128]{3,2,1,0:T(8,128)} %get-tuple-element.239) | copy-start | bytes 9437188 | tf_op jit(solution)/shard_map/while/body/eval_jaxpr/cond
  65.4 1.7 %copy-start.1 = (f32[2,8,384,128]{3,2,1,0:T(8,128)}, f32[2,8,384,128]{3,2,1,0:T(8,128)S(1)}, u32[]{:S(2)}) copy-start(f32[2,8,384,128]{3,2,1,0:T(8,128)S(1)} %multiply_add_fusion) | copy-start | bytes 9437188 | tf_op jit(solution)/shard_map/while/body/eval_jaxpr/cond
  71.4 2.3 %copy-start = (f32[2,8,384,128]{3,2,1,0:T(8,128)S(1)}, f32[2,8,384,128]{3,2,1,0:T(8,128)}, u32[]{:S(2)}) copy-start(f32[2,8,384,128]{3,2,1,0:T(8,128)} %get-tuple-element.239) | copy-start | bytes 9437188 | tf_op jit(solution)/shard_map/while/body/eval_jaxpr/cond
  77.6 1.7 %copy-start.1 = (f32[2,8,384,128]{3,2,1,0:T(8,128)}, f32[2,8,384,128]{3,2,1,0:T(8,128)S(1)}, u32[]{:S(2)}) copy-start(f32[2,8,384,128]{3,2,1,0:T(8,128)S(1)} %multiply_add_fusion) | copy-start | bytes 9437188 | tf_op jit(solution)/shard_map/while/body/eval_jaxpr/cond
  83.7 2.3 %copy-start = (f32[2,8,384,128]{3,2,1,0:T(8,128)S(1)}, f32[2,8,384,128]{3,2,1,0:T(8,128)}, u32[]{:S(2)}) copy-start(f32[2,8,384,128]{3,2,1,0:T(8,128)} %get-tuple-element.239) | copy-start | bytes 9437188 | tf_op jit(solution)/shard_map/while/body/eval_jaxpr/cond
  89.9 1.7 %copy-start.1 = (f32[2,8,384,128]{3,2,1,0:T(8,128)}, f32[2,8,384,128]{3,2,1,0:T(8,128)S(1)}, u32[]{:S(2)}) copy-start(f32[2,8,384,128]{3,2,1,0:T(8,128)S(1)} %multiply_add_fusion) | copy-start | bytes 9437188 | tf_op jit(solution)/shard_map/while/body/eval_jaxpr/cond
where the time goes:
time: 98.4 us; the launch traced here: 98.1 us
  blocking collectives  47 us (48%)
  local copies, waits for them, and re-layouts  18.5 us (19%)
  matrix products  16.6 us (17%)
  other arithmetic  13.2 us (13%)
  loops' own time  2.79 us (3%)
    all_gather x1, blocking collectives, per_device(): value_all = lax.all_gather(values, 'ctx', axis=0, tiled=True)  18.8 us
    all_gather x1, blocking collectives, per_device(): key_all = lax.all_gather(keys, 'ctx', axis=0, tiled=True)  17.9 us
    dot_general x3, matrix products, compute(): jnp.einsum('hgqk,khd->hgqd', weights.astype(jnp.bfloat16), value_heads, p...  11.5 us
    all_gather x1, blocking collectives, per_device(): segment_all = lax.all_gather(segment_ids, 'ctx', axis=0, tiled=True)  10.3 us
    unnamed x9, local copies, waits for them, and re-layouts  7.27 us
    reduce_sum x3, other arithmetic, compute(): new_total = row_total * factor + jnp.sum(weights, axis=-1)  6.83 us
    dot_general x3, matrix products, compute(): jnp.einsum('qhgd,khd->hgqk', query_heads, key_heads, preferred_element_ty...  5.11 us
    cond x15, local copies, waits for them, and re-layouts  4.98 us

commit v1 on v0

--- a/solution.py
+++ b/solution.py
@@ -5,6 +5,12 @@
 
 HEAD_DIM = 128
 GROUP = 8
+
+
+def in_order(parts, dim):
+    shape = list(parts.shape[1:])
+    shape[dim] *= parts.shape[0]
+    return jnp.moveaxis(parts, 0, dim).reshape(shape)
 
 
 def attend_block(
@@ -57,7 +63,19 @@
         jnp.zeros((heads_here, GROUP, row_count), jnp.float32),
         jnp.zeros((heads_here, GROUP, row_count, HEAD_DIM), jnp.float32),
     )
-    key_all = lax.all_gather(keys, "ctx", axis=0, tiled=True)
+    size = lax.axis_size("ctx")
+    pairs = [(i, (i + 1) % size) for i in range(size)]
+    back = [(b, a) for a, b in pairs]
+    lower, upper = ([], [])
+    for hop in range(size - 1):
+        if hop % 2 == 0:
+            lower.append(lax.ppermute(lower[-1] if lower else keys, "ctx", pairs))
+        else:
+            upper.append(lax.ppermute(upper[-1] if upper else keys, "ctx", back))
+    tiles = jnp.stack([*lower[::-1], keys, *upper])
+    shift = lax.axis_index("ctx") - len(lower)
+    tiles = tiles[(jnp.arange(size) - shift) % size]
+    key_all = in_order(tiles, 0)
     value_all = lax.all_gather(values, "ctx", axis=0, tiled=True)
     segment_all = lax.all_gather(segment_ids, "ctx", axis=0, tiled=True)
     blocks = max(1, key_all.shape[0] // row_count)

time: 98.4 us -> 92.4 us (0.939)
  blocking collectives: 47 us -> 32.2 us
  starting transfers between devices: 0 us -> 4.42 us
  waiting for transfers between devices: 0 us -> 3.47 us
  local copies, waits for them, and re-layouts: 18.5 us -> 17.2 us
  other arithmetic: 13.2 us -> 14.4 us
    all_gather x1 -> x0, blocking collectives: 17.9 us -> none  [per_device(): key_all = lax.all_gather(keys, 'ctx', axis=0, tiled=True)]
    ppermute x0 -> x3, starting transfers between devices: none -> 4.42 us  [the longest x2 3.97 us: per_device(): lower.append(lax.ppermute(lower[-1] if lower else keys, 'ctx', pairs))]
    all_gather x1, blocking collectives: 10.3 us -> 14.4 us  [per_device(): segment_all = lax.all_gather(segment_ids, 'ctx', axis=0, tiled=True)]
    ppermute x0 -> x3, waiting for transfers between devices: none -> 3.47 us  [the longest x2 3.47 us: per_device(): lower.append(lax.ppermute(lower[-1] if lower else keys, 'ctx', pairs))]
    dynamic_slice x3, local copies, waits for them, and re-layouts: 3.21 us -> 0.15 us  [turn(): value_part = lax.dynamic_slice_in_dim(value_all, offset, width_rows, 0)]
    gather x0 -> x1, local copies, waits for them, and re-layouts: none -> 1.48 us  [per_device(): tiles = tiles[(jnp.arange(size) - shift) % size]]
    reshape x0 -> x1, local copies, waits for them, and re-layouts: none -> 1.41 us  [in_order(): return jnp.moveaxis(parts, 0, dim).reshape(shape)]
    another operation x0 -> x1, other arithmetic: none -> 1.12 us  [per_device(): tiles = jnp.stack([*lower[::-1], keys, *upper])]
  transfers between devices with their start and end apart: 0 -> 3, of which waited for: 0 -> 1; matrix products, arithmetic and copies ran while one was open for 0% -> 5% of each run, Pallas kernels for 0% -> 0%
where the time goes in v1:
time: 92.4 us; the launch traced here: 91.2 us
  blocking collectives  32.2 us (35%)
  local copies, waits for them, and re-layouts  17.2 us (19%)
  matrix products  16.6 us (18%)
  other arithmetic  14.4 us (16%)
  starting transfers between devices  4.42 us (5%)
  waiting for transfers between devices  3.47 us (4%)
  loops' own time  2.85 us (3%)
    all_gather x1, blocking collectives, per_device(): value_all = lax.all_gather(values, 'ctx', axis=0, tiled=True)  17.8 us
    all_gather x1, blocking collectives, per_device(): segment_all = lax.all_gather(segment_ids, 'ctx', axis=0, tiled=True)  14.4 us
    dot_general x3, matrix products, compute(): jnp.einsum('hgqk,khd->hgqd', weights.astype(jnp.bfloat16), value_heads, p...  11.5 us
    reduce_sum x3, other arithmetic, compute(): new_total = row_total * factor + jnp.sum(weights, axis=-1)  6.83 us
    unnamed x10, local copies, waits for them, and re-layouts  6.18 us
    dot_general x3, matrix products, compute(): jnp.einsum('qhgd,khd->hgqk', query_heads, key_heads, preferred_element_ty...  5.11 us
    cond x15, local copies, waits for them, and re-layouts  4.97 us
    ppermute x2, starting transfers between devices, per_device(): lower.append(lax.ppermute(lower[-1] if lower else keys, 'ctx', pairs))  3.97 us
  transfers between devices with their start and end apart: 3, of which 1 were waited for; matrix products, arithmetic and copies ran while one was open for 5% of the time, Pallas kernels for 0%

profile of v1, /device:TPU:22, one launch (start us, length us, event | category | flops | bytes accessed | tf_op | source)
XLA Modules:
  0.0 91.2 jit_solution(15544225637767907696)
XLA Ops:
  0.0 1.6 %collective-permute-start = (bf16[384,256]{1,0:T(8,128)(2,1)}, bf16[384,256]{1,0:T(8,128)(2,1)}, u32[]{:S(2)}, u32[]{:S(2)}) collective-permute-start(bf16[384,256]{1,0:T(8,128)(2,1)} %param.9), channel_id=1, source_target_pairs={{0,4},{4,8},{8,12},{12,0},{1,5},{5,9},{9,13},{13,1},{2,6},{6,10},{... | collective-permute-start | bytes 589832 | tf_op jit(solution)/shard_map/ppermute | solution.py:72
  1.6 0.4 collective-permute-start.2
  2.0 0.7 reshape.100
  2.7 14.4 %all-gather = s32[4,1,384]{2,1,0:T(1,128)S(1)} all-gather(s32[1,1,384]{2,1,0:T(1,128)S(1)} %reshape.100), channel_id=1, replica_groups=mesh['groups'=2,'ctx'=4,'tp'=2,'sub'=2] {'ctx'}, dimensions={0}, use_global_device_ids=true | all-gather | bytes 7680 | tf_op jit(solution)/shard_map/all_gather | solution.py:80
  17.2 1.1 %copy.20 = bf16[384,256]{0,1:T(8,128)(2,1)S(1)} copy(bf16[384,256]{1,0:T(8,128)(2,1)} %param.10) | data formatting | bytes 393216 | tf_op args[2]
  18.3 1.9 %copy.19 = bf16[384,2048]{0,1:T(8,128)(2,1)S(1)} copy(bf16[384,2048]{1,0:T(8,128)(2,1)} %param.8) | data formatting | bytes 3145728 | tf_op args[0]
  20.2 1.0 %copy.21 = bf16[384,2,8,128]{3,0,2,1:T(8,128)(2,1)S(1)} copy(bf16[384,2,8,128]{0,3,2,1:T(8,128)(2,1)S(1)} %bitcast.43) | data formatting | bytes 3145728
  21.1 0.0 copy-start.3
  21.2 17.8 %all_gather.7 = bf16[1536,256]{0,1:T(8,128)(2,1)S(1)} all-gather(bf16[384,256]{0,1:T(8,128)(2,1)S(1)} %copy.20), channel_id=1, replica_groups=mesh['groups'=2,'ctx'=4,'tp'=2,'sub'=2] {'ctx'}, dimensions={0}, use_global_device_ids=true | all-gather | bytes 983040 | tf_op jit(solution)/shard_map/all_gather | solution.py:79
  38.9 2.4 %collective-permute-start.1 = (bf16[384,256]{1,0:T(8,128)(2,1)}, bf16[384,256]{1,0:T(8,128)(2,1)S(1)}, u32[]{:S(2)}, u32[]{:S(2)}) collective-permute-start(bf16[384,256]{1,0:T(8,128)(2,1)} %collective-permute-done), channel_id=1, source_target_pairs={{0,4},{4,8},{8,12},{12,0},{1,5},{5,9},{9,13},{13,1},{2,6},{6,10},{... | collective-permute-start | bytes 589832 | tf_op jit(solution)/shard_map/ppermute | solution.py:72
  41.4 3.5 %collective-permute-done.1 = bf16[384,256]{1,0:T(8,128)(2,1)S(1)} collective-permute-done((bf16[384,256]{1,0:T(8,128)(2,1)}, bf16[384,256]{1,0:T(8,128)(2,1)S(1)}, u32[]{:S(2)}, u32[]{:S(2)}) %collective-permute-start.1) | collective-permute-done | bytes 196640 | tf_op jit(solution)/shard_map/ppermute | solution.py:72
  44.8 1.1 %pad_maximum_fusion = bf16[4,384,256]{2,1,0:T(8,128)(2,1)S(1)} fusion(bf16[1,384,256]{2,1,0:T(8,128)(2,1)} %bitcast.8, bf16[1,384,256]{2,1,0:T(8,128)(2,1)S(1)} %bitcast.46, bf16[1,384,256]{2,1,0:T(8,128)(2,1)} %bitcast.6, bf16[1,384,256]{2,1,0:T(8,128)(2,1)S(1)} %bitcast.47), kind=kLoop, calls=%fused_computation.24 | loop fusion | flops 1179648 | bytes 1572864 | tf_op jit(solution)/shard_map/stack | solution.py:75
  45.9 1.5 %gather_fusion = bf16[4,384,256]{2,1,0:T(8,128)(2,1)} fusion(bf16[4,384,256]{2,1,0:T(8,128)(2,1)S(1)} %pad_maximum_fusion, s32[1024]{0:T(1024)S(1)} %pad_clamp_fusion), kind=kCustom, calls=%fused_computation | custom fusion | bytes 1572880 | tf_op jit(solution)/shard_map/gather | solution.py:77
  47.4 1.4 %copy.30 = bf16[1536,256]{0,1:T(8,128)(2,1)S(1)} copy(bf16[1536,256]{1,0:T(8,128)(2,1)} %bitcast.45) | data formatting | bytes 1572864 | tf_op jit(solution)/shard_map/reshape | solution.py:13
  48.9 2.0 %broadcast_in_dim.54 = f32[2,8,384,128]{3,2,1,0:T(8,128)} broadcast(f32[]{:T(128)} %constant.84.clone.1), dimensions={} | broadcast | bytes 3145732 | tf_op jit(solution)/shard_map/broadcast_in_dim | solution.py:64
  50.8 35.4 %while.18 = (s32[]{:T(128)}, f32[2,8,384]{2,1,0:T(8,128)S(1)}, f32[2,8,384]{2,1,0:T(8,128)S(1)}, f32[2,8,384,128]{3,2,1,0:T(8,128)}, s32[1536]{0:T(1024)S(1)}, /...) while((s32[]{:T(128)}, f32[2,8,384]{2,1,0:T(8,128)S(1)}, ...), condition=%wide.region_6.7_spmd.clone, body=%wide.region_0.6_spmd.clone.sunk | while | flops 1240953984 | bytes 63517816 | solution.py:100
  50.8 0.1 broadcast_compare_fusion.2
  50.9 0.9 fusion.21
  52.5 9.6 %conditional.3 = ((f32[2,8,384]{2,1,0:T(8,128)S(1)}, f32[2,8,384]{2,1,0:T(8,128)S(1)}, f32[2,8,384,128]{3,2,1,0:T(8,128)})) conditional(s32[]{:T(128)} %convert_element_type.33, (f32[2,8,384]{2,1,0:T(8,128)S(1)}, f32[2,8,384]{2,1,0:T(8,128)S(1)}, f32[2,8,384,128]{3,2,1,0:T(8,128)}) %tuple.60, (pred[384,384]{0,1:T(8,128)(4,1)S(1)}, ...), branch_computations={%region_2.2_spmd, %region_3.5_spmd} | conditional | flops 1240215552 | bytes 63357020 | solution.py:52
  52.5 0.1 constant_dynamic-slice_fusion
  52.5 1.7 %fusion.2 = (f32[2,8,384]{2,1,0:T(8,128)S(1)}, f32[2,384,384,8]{2,1,3,0:T(8,128)S(1)}) fusion(pred[384,384]{0,1:T(8,128)(4,1)S(1)} %get-tuple-element.234, bf16[384,2,128,1]{0,2,3,1:T(8,128)(2,1)S(1)} %bitcast.41, bf16[384,2,8,128]{3,0,2,1:T(8,128)(2,1)S(1)} %get-tuple-element.237), kind=kOutput, calls=%fused_computation.4 | convolution fusion | flops 611051520 | bytes 11378688 | tf_op jit(solution)/shard_map/while/body/eval_jaxpr/cond/branch_1_fun/qhgd,khd->hgqk/dot_general | solution.py:36
  54.3 0.0 copy-start
  54.3 2.3 %fusion.4 = f32[2,8,384]{2,1,0:T(8,128)S(1)} fusion(f32[2,384,384,8]{2,1,3,0:T(8,128)S(1)} %get-tuple-element.332, f32[2,8,384]{2,1,0:T(8,128)S(1)} %max.4, pred[384,384]{0,1:T(8,128)(4,1)S(1)} %get-tuple-element.234), kind=kLoop, calls=%fused_computation.6 | loop fusion | flops 11790336 | bytes 9633792 | tf_op jit(solution)/shard_map/while/body/eval_jaxpr/cond/branch_1_fun/reduce_sum | solution.py:43
  56.6 3.8 %multiply_add_fusion = f32[2,8,384,128]{3,2,1,0:T(8,128)S(1)} fusion(f32[2,8,384,128]{3,2,1,0:T(8,128)S(1)} %copy-done, bf16[384,2,128,1]{0,2,3,1:T(8,128)(2,1)S(1)} %bitcast.44, f32[2,384,384,8]{2,1,3,0:T(8,128)S(1)} %get-tuple-element.332, f32[2,8,384]{2,1,0:T(8,128)S(1)} %max.4, pred[384,384]{0,1:T(8,128)(4,1)S(1)} %get-tuple-element.234, ...), kind=kOutput, calls=%fused_computation.9 | convolution fusion | flops 617349120 | bytes 16121856 | tf_op jit(solution)/shard_map/while/body/eval_jaxpr/cond/branch_1_fun/hgqk,khd->hgqd/dot_general | solution.py:44
  60.5 1.6 %copy-done.1 = f32[2,8,384,128]{3,2,1,0:T(8,128)} copy-done((f32[2,8,384,128]{3,2,1,0:T(8,128)}, f32[2,8,384,128]{3,2,1,0:T(8,128)S(1)}, u32[]{:S(2)}) %copy-start.1) | copy-done | bytes 3145752 | tf_op jit(solution)/shard_map/while/body/eval_jaxpr/cond
  62.1 0.1 broadcast_compare_fusion.2
  62.2 0.9 fusion.21
  63.7 9.6 %conditional.3 = ((f32[2,8,384]{2,1,0:T(8,128)S(1)}, f32[2,8,384]{2,1,0:T(8,128)S(1)}, f32[2,8,384,128]{3,2,1,0:T(8,128)})) conditional(s32[]{:T(128)} %convert_element_type.33, (f32[2,8,384]{2,1,0:T(8,128)S(1)}, f32[2,8,384]{2,1,0:T(8,128)S(1)}, f32[2,8,384,128]{3,2,1,0:T(8,128)}) %tuple.60, (pred[384,384]{0,1:T(8,128)(4,1)S(1)}, ...), branch_computations={%region_2.2_spmd, %region_3.5_spmd} | conditional | flops 1240215552 | bytes 63357020 | solution.py:52
  63.7 0.1 constant_dynamic-slice_fusion
  63.8 1.7 %fusion.2 = (f32[2,8,384]{2,1,0:T(8,128)S(1)}, f32[2,384,384,8]{2,1,3,0:T(8,128)S(1)}) fusion(pred[384,384]{0,1:T(8,128)(4,1)S(1)} %get-tuple-element.234, bf16[384,2,128,1]{0,2,3,1:T(8,128)(2,1)S(1)} %bitcast.41, bf16[384,2,8,128]{3,0,2,1:T(8,128)(2,1)S(1)} %get-tuple-element.237), kind=kOutput, calls=%fused_computation.4 | convolution fusion | flops 611051520 | bytes 11378688 | tf_op jit(solution)/shard_map/while/body/eval_jaxpr/cond/branch_1_fun/qhgd,khd->hgqk/dot_general | solution.py:36
  65.5 0.0 copy-start
  65.5 2.3 %fusion.4 = f32[2,8,384]{2,1,0:T(8,128)S(1)} fusion(f32[2,384,384,8]{2,1,3,0:T(8,128)S(1)} %get-tuple-element.332, f32[2,8,384]{2,1,0:T(8,128)S(1)} %max.4, pred[384,384]{0,1:T(8,128)(4,1)S(1)} %get-tuple-element.234), kind=kLoop, calls=%fused_computation.6 | loop fusion | flops 11790336 | bytes 9633792 | tf_op jit(solution)/shard_map/while/body/eval_jaxpr/cond/branch_1_fun/reduce_sum | solution.py:43
  67.9 3.8 %multiply_add_fusion = f32[2,8,384,128]{3,2,1,0:T(8,128)S(1)} fusion(f32[2,8,384,128]{3,2,1,0:T(8,128)S(1)} %copy-done, bf16[384,2,128,1]{0,2,3,1:T(8,128)(2,1)S(1)} %bitcast.44, f32[2,384,384,8]{2,1,3,0:T(8,128)S(1)} %get-tuple-element.332, f32[2,8,384]{2,1,0:T(8,128)S(1)} %max.4, pred[384,384]{0,1:T(8,128)(4,1)S(1)} %get-tuple-element.234, ...), kind=kOutput, calls=%fused_computation.9 | convolution fusion | flops 617349120 | bytes 16121856 | tf_op jit(solution)/shard_map/while/body/eval_jaxpr/cond/branch_1_fun/hgqk,khd->hgqd/dot_general | solution.py:44
  71.7 1.6 %copy-done.1 = f32[2,8,384,128]{3,2,1,0:T(8,128)} copy-done((f32[2,8,384,128]{3,2,1,0:T(8,128)}, f32[2,8,384,128]{3,2,1,0:T(8,128)S(1)}, u32[]{:S(2)}) %copy-start.1) | copy-done | bytes 3145752 | tf_op jit(solution)/shard_map/while/body/eval_jaxpr/cond
  73.4 0.1 broadcast_compare_fusion.2
  73.4 0.9 fusion.21
  75.0 9.6 %conditional.3 = ((f32[2,8,384]{2,1,0:T(8,128)S(1)}, f32[2,8,384]{2,1,0:T(8,128)S(1)}, f32[2,8,384,128]{3,2,1,0:T(8,128)})) conditional(s32[]{:T(128)} %convert_element_type.33, (f32[2,8,384]{2,1,0:T(8,128)S(1)}, f32[2,8,384]{2,1,0:T(8,128)S(1)}, f32[2,8,384,128]{3,2,1,0:T(8,128)}) %tuple.60, (pred[384,384]{0,1:T(8,128)(4,1)S(1)}, ...), branch_computations={%region_2.2_spmd, %region_3.5_spmd} | conditional | flops 1240215552 | bytes 63357020 | solution.py:52
  75.0 0.1 constant_dynamic-slice_fusion
  75.1 1.7 %fusion.2 = (f32[2,8,384]{2,1,0:T(8,128)S(1)}, f32[2,384,384,8]{2,1,3,0:T(8,128)S(1)}) fusion(pred[384,384]{0,1:T(8,128)(4,1)S(1)} %get-tuple-element.234, bf16[384,2,128,1]{0,2,3,1:T(8,128)(2,1)S(1)} %bitcast.41, bf16[384,2,8,128]{3,0,2,1:T(8,128)(2,1)S(1)} %get-tuple-element.237), kind=kOutput, calls=%fused_computation.4 | convolution fusion | flops 611051520 | bytes 11378688 | tf_op jit(solution)/shard_map/while/body/eval_jaxpr/cond/branch_1_fun/qhgd,khd->hgqk/dot_general | solution.py:36
  76.8 0.0 copy-start
  76.8 2.3 %fusion.4 = f32[2,8,384]{2,1,0:T(8,128)S(1)} fusion(f32[2,384,384,8]{2,1,3,0:T(8,128)S(1)} %get-tuple-element.332, f32[2,8,384]{2,1,0:T(8,128)S(1)} %max.4, pred[384,384]{0,1:T(8,128)(4,1)S(1)} %get-tuple-element.234), kind=kLoop, calls=%fused_computation.6 | loop fusion | flops 11790336 | bytes 9633792 | tf_op jit(solution)/shard_map/while/body/eval_jaxpr/cond/branch_1_fun/reduce_sum | solution.py:43
  79.1 3.8 %multiply_add_fusion = f32[2,8,384,128]{3,2,1,0:T(8,128)S(1)} fusion(f32[2,8,384,128]{3,2,1,0:T(8,128)S(1)} %copy-done, bf16[384,2,128,1]{0,2,3,1:T(8,128)(2,1)S(1)} %bitcast.44, f32[2,384,384,8]{2,1,3,0:T(8,128)S(1)} %get-tuple-element.332, f32[2,8,384]{2,1,0:T(8,128)S(1)} %max.4, pred[384,384]{0,1:T(8,128)(4,1)S(1)} %get-tuple-element.234, ...), kind=kOutput, calls=%fused_computation.9 | convolution fusion | flops 617349120 | bytes 16121856 | tf_op jit(solution)/shard_map/while/body/eval_jaxpr/cond/branch_1_fun/hgqk,khd->hgqd/dot_general | solution.py:44
  83.0 1.6 %copy-done.1 = f32[2,8,384,128]{3,2,1,0:T(8,128)} copy-done((f32[2,8,384,128]{3,2,1,0:T(8,128)}, f32[2,8,384,128]{3,2,1,0:T(8,128)S(1)}, u32[]{:S(2)}) %copy-start.1) | copy-done | bytes 3145752 | tf_op jit(solution)/shard_map/while/body/eval_jaxpr/cond
  84.6 0.1 broadcast_compare_fusion.2
  84.7 0.9 fusion.21
  86.3 2.4 %fusion.13 = bf16[384,2,8,128]{3,0,2,1:T(8,128)(2,1)S(1)} fusion(f32[2,8,384,128]{3,2,1,0:T(8,128)} %get-tuple-element.257, f32[2,8,384]{2,1,0:T(8,128)S(1)} %get-tuple-element.258), kind=kLoop, calls=%fused_computation.23 | loop fusion | flops 1572864 | bytes 4743168 | tf_op jit(solution)/shard_map/convert_element_type | solution.py:104
  88.7 1.0 %copy.22 = bf16[384,2,8,128]{3,2,1,0:T(8,128)(2,1)S(1)} copy(bf16[384,2,8,128]{3,0,2,1:T(8,128)(2,1)S(1)} %fusion.13) | data formatting | bytes 3145728 | tf_op jit(solution)/shard_map/convert_element_type | solution.py:104
  89.7 1.6 %copy.33 = bf16[48,8,16,128]{3,1,2,0:T(8,128)(2,1)} copy(bf16[48,8,16,128]{3,2,1,0:T(8,128)(2,1)S(1)} %bitcast.42) | data formatting | bytes 3145728
  (31 shorter events, 0.2 us)
Async XLA Ops:
  0.0 44.8 %copy-start.2 = (bf16[384,256]{1,0:T(8,128)(2,1)S(1)}, bf16[384,256]{1,0:T(8,128)(2,1)}, u32[]{:S(2)}) copy-start(bf16[384,256]{1,0:T(8,128)(2,1)} %param.9) | copy-start | bytes 589828
  0.0 38.9 %collective-permute-start = (bf16[384,256]{1,0:T(8,128)(2,1)}, bf16[384,256]{1,0:T(8,128)(2,1)}, u32[]{:S(2)}, u32[]{:S(2)}) collective-permute-start(bf16[384,256]{1,0:T(8,128)(2,1)} %param.9), channel_id=1, source_target_pairs={{0,4},{4,8},{8,12},{12,0},{1,5},{5,9},{9,13},{13,1},{2,6},{6,10},{... | collective-permute-start | bytes 589832 | tf_op jit(solution)/shard_map/ppermute | solution.py:72
  1.6 39.8 %collective-permute-start.2 = (bf16[384,256]{1,0:T(8,128)(2,1)}, bf16[384,256]{1,0:T(8,128)(2,1)}, u32[]{:S(2)}, u32[]{:S(2)}) collective-permute-start(bf16[384,256]{1,0:T(8,128)(2,1)} %param.9), channel_id=1, source_target_pairs={{4,0},{8,4},{12,8},{0,12},{5,1},{9,5},{13,9},{1,13},{6,2},{10,6},{... | collective-permute-start | bytes 589832 | tf_op jit(solution)/shard_map/ppermute | solution.py:74
  21.1 29.7 %copy-start.3 = (s32[384]{0:T(512)S(1)}, s32[384]{0:T(512)}, u32[]{:S(2)}) copy-start(s32[384]{0:T(512)} %param.11) | copy-start | bytes 4612
  38.9 5.9 %collective-permute-start.1 = (bf16[384,256]{1,0:T(8,128)(2,1)}, bf16[384,256]{1,0:T(8,128)(2,1)S(1)}, u32[]{:S(2)}, u32[]{:S(2)}) collective-permute-start(bf16[384,256]{1,0:T(8,128)(2,1)} %collective-permute-done), channel_id=1, source_target_pairs={{0,4},{4,8},{8,12},{12,0},{1,5},{5,9},{9,13},{13,1},{2,6},{6,10},{... | collective-permute-start | bytes 589832 | tf_op jit(solution)/shard_map/ppermute | solution.py:72
  54.3 2.3 %copy-start = (f32[2,8,384,128]{3,2,1,0:T(8,128)S(1)}, f32[2,8,384,128]{3,2,1,0:T(8,128)}, u32[]{:S(2)}) copy-start(f32[2,8,384,128]{3,2,1,0:T(8,128)} %get-tuple-element.239) | copy-start | bytes 9437188 | tf_op jit(solution)/shard_map/while/body/eval_jaxpr/cond
  60.4 1.7 %copy-start.1 = (f32[2,8,384,128]{3,2,1,0:T(8,128)}, f32[2,8,384,128]{3,2,1,0:T(8,128)S(1)}, u32[]{:S(2)}) copy-start(f32[2,8,384,128]{3,2,1,0:T(8,128)S(1)} %multiply_add_fusion) | copy-start | bytes 9437188 | tf_op jit(solution)/shard_map/while/body/eval_jaxpr/cond
  65.5 2.3 %copy-start = (f32[2,8,384,128]{3,2,1,0:T(8,128)S(1)}, f32[2,8,384,128]{3,2,1,0:T(8,128)}, u32[]{:S(2)}) copy-start(f32[2,8,384,128]{3,2,1,0:T(8,128)} %get-tuple-element.239) | copy-start | bytes 9437188 | tf_op jit(solution)/shard_map/while/body/eval_jaxpr/cond
  71.7 1.7 %copy-start.1 = (f32[2,8,384,128]{3,2,1,0:T(8,128)}, f32[2,8,384,128]{3,2,1,0:T(8,128)S(1)}, u32[]{:S(2)}) copy-start(f32[2,8,384,128]{3,2,1,0:T(8,128)S(1)} %multiply_add_fusion) | copy-start | bytes 9437188 | tf_op jit(solution)/shard_map/while/body/eval_jaxpr/cond
  76.8 2.3 %copy-start = (f32[2,8,384,128]{3,2,1,0:T(8,128)S(1)}, f32[2,8,384,128]{3,2,1,0:T(8,128)}, u32[]{:S(2)}) copy-start(f32[2,8,384,128]{3,2,1,0:T(8,128)} %get-tuple-element.239) | copy-start | bytes 9437188 | tf_op jit(solution)/shard_map/while/body/eval_jaxpr/cond
  82.9 1.7 %copy-start.1 = (f32[2,8,384,128]{3,2,1,0:T(8,128)}, f32[2,8,384,128]{3,2,1,0:T(8,128)S(1)}, u32[]{:S(2)}) copy-start(f32[2,8,384,128]{3,2,1,0:T(8,128)S(1)} %multiply_add_fusion) | copy-start | bytes 9437188 | tf_op jit(solution)/shard_map/while/body/eval_jaxpr/cond
